TPU v7x, 32 devices: a whole 2x2x4 slice. The times are simulated.
32 devices in a mesh: rep: 16 (over z, x, core), fsdp: 2 (over y).
Axes of the slice: x: 2, y: 2, z: 4, core: 2. Of those that a mesh axis runs over, the one named last changes fastest.
Arguments:
- gradients: bfloat16 [16, 4, 64, 4096], P('rep', None, 'fsdp'), may hold values from -8000 to 8000
- local_params: float32 [16, 4, 64, 4096], P('rep', None, 'fsdp'), may hold values from -6 to 6
- first_moment: float32 [16, 4, 64, 4096], P('rep', None, 'fsdp'), may hold values from -6 to 6
- second_moment: float32 [16, 4, 64, 4096], P('rep', None, 'fsdp'), may hold values from 0.05 to 2
- global_params: float32 [4, 64, 4096], P(None, 'fsdp'), may hold values from -6 to 6
- outer_momentum: float32 [4, 64, 4096], P(None, 'fsdp'), may hold values from -6 to 6
Outputs:
- new_global: float32 [4, 64, 4096], P(None, 'fsdp')
- new_momentum: float32 [4, 64, 4096], P(None, 'fsdp')
- new_first: float32 [16, 4, 64, 4096], P('rep', None, 'fsdp')
- new_second: float32 [16, 4, 64, 4096], P('rep', None, 'fsdp')
All inputs are finite; a program needn't handle non-finite values.
Results may differ from a plain program's by a relative error of at most 0.0003.
Values sent between devices are 32-bit elements; how exact they have to be, the bound alone decides.
A program may use at most 128 MiB of HBM per device.

v0:
```python
import jax
import jax.numpy as jnp
from jax import lax
from jax.sharding import PartitionSpec as P

STEP = 20


def outer_step(delta, global_now, momentum_now, replicas):
    pseudo = lax.psum(delta, "rep") / replicas
    momentum_next = 0.9 * momentum_now + pseudo
    global_next = global_now - 0.7 * (pseudo + 0.9 * momentum_next)
    return (global_next, momentum_next)


def on_device(gradients, local_params, first_moment, second_moment, global_params, outer_momentum):
    first_fix = 1.0 - 0.9**STEP
    second_fix = 1.0 - 0.95**STEP
    gradient = gradients[0].astype(jnp.float32)
    squares = lax.psum(jnp.sum(gradient * gradient), "fsdp")
    count_all = gradient.size * lax.axis_size("fsdp")
    factor = jnp.minimum(1.0, 0.5 / jnp.sqrt(squares / count_all))
    replicas = lax.axis_size("rep")
    firsts, seconds, deltas, globals_new, momenta_new = ([], [], [], [], [])
    for matrix in range(gradient.shape[0]):
        clipped = gradient[matrix] * factor
        first_new = 0.9 * first_moment[0, matrix] + 0.1 * clipped
        second_new = 0.95 * second_moment[0, matrix] + 0.05 * clipped * clipped
        update = first_new / first_fix / (jnp.sqrt(second_new / second_fix) + 1e-08)
        local_now = local_params[0, matrix]
        stepped = local_now - 0.1 * (update + 0.1 * local_now)
        delta = global_params[matrix] - stepped
        first_new, second_new, delta = (first_new, second_new, delta)
        firsts.append(first_new)
        seconds.append(second_new)
        global_next, momentum_next = outer_step(
            delta[None],
            global_params[matrix : matrix + 1],
            outer_momentum[matrix : matrix + 1],
            replicas,
        )
        globals_new.append(global_next)
        momenta_new.append(momentum_next)
    global_all = jnp.concatenate(globals_new, axis=0)
    momentum_all = jnp.concatenate(momenta_new, axis=0)
    return (global_all, momentum_all, jnp.stack(firsts)[None], jnp.stack(seconds)[None])


def solution(mesh):
    placed = (
        P("rep", None, "fsdp", None),
        P("rep", None, "fsdp", None),
        P("rep", None, "fsdp", None),
        P("rep", None, "fsdp", None),
        P(None, "fsdp", None),
        P(None, "fsdp", None),
    )
    return jax.shard_map(
        on_device,
        mesh=mesh,
        in_specs=placed,
        out_specs=(
            P(None, "fsdp", None),
            P(None, "fsdp", None),
            P("rep", None, "fsdp", None),
            P("rep", None, "fsdp", None),
        ),
        check_vma=False,
    )
```

profile of v0, /device:TPU:0, one launch (start us, length us, event | category | flops | bytes accessed | tf_op | source)
XLA Modules:
  0.0 139.5 jit_solution(10752124649814436725)
XLA Ops:
  7.2 0.0 copy-start
  7.2 0.0 all-reduce.3.cloned.1.call-start
  7.2 2.5 %multiply_reduce_fusion = f32[]{:T(128)} fusion(bf16[1,4,32,4096]{3,2,1,0:T(8,128)(2,1)} %param.6), kind=kLoop, calls=%fused_computation.4 | loop fusion | flops 1572863 | bytes 1048580 | tf_op jit(solution)/shard_map/reduce_sum | solution.py:20
  9.7 2.8 %convert_element_type.4 = f32[1,4,32,4096]{3,2,1,0:T(8,128)} convert(bf16[1,4,32,4096]{3,2,1,0:T(8,128)(2,1)} %param.6) | non-fusion elementwise | flops 524288 | bytes 3145728 | tf_op jit(solution)/shard_map/convert_element_type | solution.py:19
  12.5 6.5 %psum.35 = f32[]{:T(128)} all-reduce(f32[]{:T(128)} %multiply_reduce_fusion), channel_id=1, replica_groups=mesh['rep'=16,'fsdp'=2] {'fsdp'}, use_global_device_ids=true, to_apply=%region_1.0 | all-reduce | flops 1 | bytes 8 | tf_op jit(solution)/shard_map/psum | solution.py:20
  19.7 0.0 copy-done
  19.7 0.0 copy-start.1
  19.7 0.0 copy-start.2
  19.7 2.9 %fusion.13 = (f32[1,32,4096]{2,1,0:T(8,128)}, f32[1,32,4096]{2,1,0:T(8,128)S(1)}, f32[1,32,4096]{2,1,0:T(8,128)S(1)}) fusion(f32[1,4,32,4096]{3,2,1,0:T(8,128)} %param.7, f32[4,32,4096]{2,1,0:T(8,128)S(1)} %copy-done, f32[]{:T(128)S(6)} %min_shard_map.3, f32[1,4,32,4096]{3,2,1,0:T(8,128)} %convert_element_type.4, f32[1,4,32,4096]{3,2,1,0:T(8,128)} %param.8, ...), kind=kLoop, calls=%fused_computation.32 | loop fusion | flops 2228224 | bytes 4194308 | tf_op jit(solution)/shard_map/sub | solution.py:32
  22.6 0.0 copy-done.1
  22.6 0.0 copy-done.2
  22.6 4.5 %fusion.19 = (f32[1,32,4096]{2,1,0:T(8,128)}, f32[1,32,4096]{2,1,0:T(8,128)}, f32[1,32,4096]{2,1,0:T(8,128)}, f32[1,32,4096]{2,1,0:T(8,128)}, f32[1,32,4096]{2,1...) fusion(f32[1,4,32,4096]{3,2,1,0:T(8,128)S(1)} %copy-done.2, ...), kind=kLoop, calls=%fused_computation.44 | loop fusion | flops 6684672 | bytes 12582916 | tf_op jit(solution)/shard_map/sub | solution.py:32
  27.2 0.0 all-reduce.3.cloned.1.call-update
  27.2 4.2 %maximum_bitcast_fusion = (f32[1,4,32,4096]{3,2,1,0:T(8,128)}, f32[1,4,32,4096]{3,2,1,0:T(8,128)}) fusion(f32[1,32,4096]{2,1,0:T(8,128)} %get-tuple-element.25, f32[1,32,4096]{2,1,0:T(8,128)S(1)} %get-tuple-element.15, f32[1,32,4096]{2,1,0:T(8,128)} %get-tuple-element.22, f32[1,32,4096]{2,1,0:T(8,128)} %get-tuple-element.9, ...), kind=kLoop, calls=%fused_computation.2 | loop fusion | flops 3145728 | bytes 8388608 | tf_op jit(solution)/shard_map/broadcast_in_dim | solution.py:46
  31.4 96.0 %all-reduce.3.cloned.1.call-done = (f32[1,32,4096]{2,1,0:T(8,128)}, f32[1,32,4096]{2,1,0:T(8,128)}, f32[1,32,4096]{2,1,0:T(8,128)}, f32[1,32,4096]{2,1,0:T(8,128)}) async-done(((f32[1,32,4096]{2,1,0:T(8,128)}, f32[1,32,4096]{2,1,0:T(8,128)}, f32[1,32,4096]{2,1,0:T(8,128)}, f32[1,32,4096]{2,1,0:T(8,128)}), (f32[1,32,4096]{2,1,0:T(8,128)}, f32[1,32,4096]{2,1,0:T(8,128)}, f32[1,32,4096]{2,1,0:T(8,128)}, ...) | async-done | bytes 2097168 | tf_op jit(solution)/shard_map/psum | solution.py:10
  127.4 2.7 %multiply_subtract_fusion.3 = (f32[1,32,4096]{2,1,0:T(8,128)S(1)}, f32[1,32,4096]{2,1,0:T(8,128)S(1)}, f32[1,32,4096]{2,1,0:T(8,128)S(1)}, f32[1,32,4096]{2,1,0:...) fusion(f32[1,32,4096]{2,1,0:T(8,128)} %get-tuple-element.7, ...), kind=kLoop, calls=%fused_computation.51 | loop fusion | flops 3670016 | bytes 10485760 | tf_op jit(solution)/shard_map/sub | solution.py:12
  130.2 2.5 %pad_maximum_fusion = (f32[4,32,4096]{2,1,0:T(8,128)}, f32[4,32,4096]{2,1,0:T(8,128)}) fusion(f32[1,32,4096]{2,1,0:T(8,128)S(1)} %get-tuple-element.29, f32[1,32,4096]{2,1,0:T(8,128)S(1)} %get-tuple-element.28, f32[1,32,4096]{2,1,0:T(8,128)S(1)} %get-tuple-element.27, f32[1,32,4096]{2,1,0:T(8,128)S(1)} %get-tuple-element.26, ...), kind=kLoop, calls=%fused_computation | loop fusion | flops 3145728 | bytes 8388608 | tf_op jit(solution)/shard_map/concatenate | solution.py:44
Async XLA Ops:
  7.2 12.5 %copy-start = (f32[4,32,4096]{2,1,0:T(8,128)S(1)}, f32[4,32,4096]{2,1,0:T(8,128)}, u32[]{:S(2)}) copy-start(f32[4,32,4096]{2,1,0:T(8,128)} %param.10) | copy-start | bytes 6291460
  7.2 120.3 %all-reduce.3.cloned.1.call-start = ((), (), s32[]{:S(2)}) async-start(), calls=%async_computation | async-start | bytes 4194304 | tf_op jit(solution)/shard_map/psum | solution.py:10
  19.7 2.9 %copy-start.1 = (f32[1,4,32,4096]{3,2,1,0:T(8,128)S(1)}, f32[1,4,32,4096]{3,2,1,0:T(8,128)}, u32[]{:S(2)}) copy-start(f32[1,4,32,4096]{3,2,1,0:T(8,128)} %convert_element_type.4) | copy-start | bytes 6291460
  19.7 2.9 %copy-start.2 = (f32[1,4,32,4096]{3,2,1,0:T(8,128)S(1)}, f32[1,4,32,4096]{3,2,1,0:T(8,128)}, u32[]{:S(2)}) copy-start(f32[1,4,32,4096]{3,2,1,0:T(8,128)} %param.7) | copy-start | bytes 6291460
Sparse Core Ops, SparseCore 0:
  27.3 100.0 all-reduce.2
where the time goes:
time: 140 us
  waiting for transfers between devices  96 us (69%)
  other arithmetic  22.2 us (16%)
  between operations  14.8 us (11%)
  blocking collectives  6.51 us (5%)
    psum x1, waiting for transfers between devices, outer_step(): pseudo = lax.psum(delta, 'rep') / replicas  96 us
    sub x2, other arithmetic, on_device(): delta = global_params[matrix] - stepped  7.45 us
    psum x1, blocking collectives, on_device(): squares = lax.psum(jnp.sum(gradient * gradient), 'fsdp')  6.51 us
    broadcast_in_dim x1, other arithmetic, on_device(): jnp.stack(firsts)[None]  4.24 us
  transfers between devices with their start and end apart: 1, of which 1 were waited for; matrix products, arithmetic and copies ran while one was open for 3% of the time, Pallas kernels for 0%

commit v1 on v0

--- a/solution.py
+++ b/solution.py
@@ -7,7 +7,7 @@
 
 
 def outer_step(delta, global_now, momentum_now, replicas):
-    pseudo = lax.psum(delta, "rep") / replicas
+    pseudo = jnp.sum(lax.all_gather(delta, "rep"), axis=0) / replicas
     momentum_next = 0.9 * momentum_now + pseudo
     global_next = global_now - 0.7 * (pseudo + 0.9 * momentum_next)
     return (global_next, momentum_next)

time: 140 us -> 340 us (2.43)
  waiting for transfers between devices: 96 us -> 280 us
  other arithmetic: 22.2 us -> 38.7 us
    all_gather x0 -> x4, waiting for transfers between devices: none -> 278 us  [outer_step(): pseudo = jnp.sum(lax.all_gather(delta, 'rep'), axis=0) / replicas]
    psum x1 -> x0, waiting for transfers between devices: 96 us -> none  [outer_step(): pseudo = lax.psum(delta, 'rep') / replicas]
    reduce_sum x0 -> x4, other arithmetic: none -> 16.9 us  [outer_step(): pseudo = jnp.sum(lax.all_gather(delta, 'rep'), axis=0) / replicas]
  transfers between devices with their start and end apart: 1 -> 4, of which waited for: 1 -> 4; matrix products, arithmetic and copies ran while one was open for 3% -> 7% of each run, Pallas kernels for 0% -> 0%
where the time goes in v1:
time: 340 us
  waiting for transfers between devices  280 us (82%)
  other arithmetic  38.7 us (11%)
  between operations  14.5 us (4%)
  blocking collectives  6.54 us (2%)
    all_gather x4, waiting for transfers between devices, outer_step(): pseudo = jnp.sum(lax.all_gather(delta, 'rep'), axis=0) / replicas  278 us
    reduce_sum x4, other arithmetic, outer_step(): pseudo = jnp.sum(lax.all_gather(delta, 'rep'), axis=0) / replicas  16.9 us
    sub x2, other arithmetic, on_device(): delta = global_params[matrix] - stepped  7.81 us
  transfers between devices with their start and end apart: 4, of which 4 were waited for; matrix products, arithmetic and copies ran while one was open for 7% of the time, Pallas kernels for 0%

profile of v1, /device:TPU:0, one launch (start us, length us, event | category | flops | bytes accessed | tf_op | source)
XLA Modules:
  0.0 339.5 jit_solution(5506320077132438437)
XLA Ops:
  7.2 0.0 all-gather.9.cloned.1.call-start
  7.2 2.4 multiply_reduce_fusion
  9.6 1.4 convert_element_type.4
  11.0 6.5 %psum.7 = f32[]{:T(128)} all-reduce(f32[]{:T(128)} %multiply_reduce_fusion), channel_id=1, replica_groups=mesh['rep'=16,'fsdp'=2] {'fsdp'}, use_global_device_ids=true, to_apply=%region_1.0 | all-reduce | flops 1 | bytes 8 | tf_op jit(solution)/shard_map/psum | solution.py:20
  18.2 2.8 bitcast_subtract_fusion.1
  21.0 0.0 all-gather.9.cloned.1.call-update
  21.0 0.0 all-gather.5.cloned.1.call-start
  21.1 5.0 %bitcast_subtract_fusion.3 = (f32[1,1,32,4096]{3,2,1,0:T(8,128)}, f32[1,1,32,4096]{3,2,1,0:T(8,128)}, f32[1,1,32,4096]{3,2,1,0:T(8,128)}) fusion(f32[1,4,32,4096]{3,2,1,0:T(8,128)} %param.7, f32[4,32,4096]{2,1,0:T(8,128)} %param.10, f32[1,4,32,4096]{3,2,1,0:T(8,128)} %param.8, f32[1,4,32,4096]{3,2,1,0:T(8,128)} %param.9, ...), kind=kLoop, calls=%fused_computation.72 | loop fusion | flops 6684672 | bytes 9437188 | tf_op jit(solution)/shard_map/sub | solution.py:32
  26.1 0.0 all-gather.5.cloned.1.call-update
  26.2 0.0 all-gather.7.cloned.1.call-start
  26.2 0.7 all-gather.7.cloned.1.call-update
  26.9 0.0 all-gather.11.cloned.1.call-start
  26.9 0.5 all-gather.11.cloned.1.call-update
  27.5 2.8 fusion.24
  30.3 2.5 maximum_bitcast_fusion
  32.8 64.5 %all-gather.9.cloned.1.call-done = f32[16,1,32,4096]{3,2,1,0:T(8,128)} async-done(((f32[1,1,32,4096]{3,2,1,0:T(8,128)}), f32[16,1,32,4096]{3,2,1,0:T(8,128)}) %all-gather.9.cloned.1.call-update) | async-done | bytes 8388624 | tf_op jit(solution)/shard_map/all_gather | solution.py:10
  97.3 3.8 %reduce_sum.48 = f32[32,4096]{1,0:T(8,128)S(1)} reduce(f32[16,1,32,4096]{3,2,1,0:T(8,128)} %all-gather.9.cloned.1.call-done, f32[]{:T(128)} %constant.29.clone.1), dimensions={0,1}, to_apply=%region_4.0 | reduce | flops 1966080 | bytes 8912900 | tf_op jit(solution)/shard_map/reduce_sum | solution.py:10
  101.1 71.8 %all-gather.5.cloned.1.call-done = f32[16,1,32,4096]{3,2,1,0:T(8,128)} async-done(((f32[1,1,32,4096]{3,2,1,0:T(8,128)}), f32[16,1,32,4096]{3,2,1,0:T(8,128)}) %all-gather.5.cloned.1.call-update) | async-done | bytes 8388624 | tf_op jit(solution)/shard_map/all_gather | solution.py:10
  172.9 3.8 %reduce_sum.46 = f32[32,4096]{1,0:T(8,128)S(1)} reduce(f32[16,1,32,4096]{3,2,1,0:T(8,128)} %all-gather.5.cloned.1.call-done, f32[]{:T(128)} %constant.29.clone.1), dimensions={0,1}, to_apply=%region_2.0 | reduce | flops 1966080 | bytes 8912900 | tf_op jit(solution)/shard_map/reduce_sum | solution.py:10
  176.7 71.8 %all-gather.7.cloned.1.call-done = f32[16,1,32,4096]{3,2,1,0:T(8,128)} async-done(((f32[1,1,32,4096]{3,2,1,0:T(8,128)}), f32[16,1,32,4096]{3,2,1,0:T(8,128)}) %all-gather.7.cloned.1.call-update) | async-done | bytes 8388624 | tf_op jit(solution)/shard_map/all_gather | solution.py:10
  248.6 4.6 %reduce_sum.47 = f32[32,4096]{1,0:T(8,128)} reduce(f32[16,1,32,4096]{3,2,1,0:T(8,128)} %all-gather.7.cloned.1.call-done, f32[]{:T(128)} %constant.29.clone.1), dimensions={0,1}, to_apply=%region_3.0 | reduce | flops 1966080 | bytes 8912900 | tf_op jit(solution)/shard_map/reduce_sum | solution.py:10
  253.2 0.0 copy-start
  253.2 70.3 %all-gather.11.cloned.1.call-done = f32[16,1,32,4096]{3,2,1,0:T(8,128)} async-done(((f32[1,1,32,4096]{3,2,1,0:T(8,128)}), f32[16,1,32,4096]{3,2,1,0:T(8,128)}) %all-gather.11.cloned.1.call-update) | async-done | bytes 8388624 | tf_op jit(solution)/shard_map/all_gather | solution.py:10
  323.5 4.6 %reduce_sum.49 = f32[32,4096]{1,0:T(8,128)} reduce(f32[16,1,32,4096]{3,2,1,0:T(8,128)} %all-gather.11.cloned.1.call-done, f32[]{:T(128)} %constant.29.clone.1), dimensions={0,1}, to_apply=%region_5.0 | reduce | flops 1966080 | bytes 8912900 | tf_op jit(solution)/shard_map/reduce_sum | solution.py:10
  328.1 0.0 copy-done
  328.1 2.4 fusion.39
  330.5 2.5 pad_maximum_fusion
Async XLA Ops:
  7.2 90.1 %all-gather.9.cloned.1.call-start = ((), (), s32[]{:S(2)}) async-start(), calls=%async_computation.2 | async-start | bytes 8912896 | tf_op jit(solution)/shard_map/all_gather | solution.py:10
  21.0 151.9 %all-gather.5.cloned.1.call-start = ((), (), s32[]{:S(2)}) async-start(), calls=%async_computation | async-start | bytes 8912896 | tf_op jit(solution)/shard_map/all_gather | solution.py:10
  26.2 222.4 %all-gather.7.cloned.1.call-start = ((), (), s32[]{:S(2)}) async-start(), calls=%async_computation.1 | async-start | bytes 8912896 | tf_op jit(solution)/shard_map/all_gather | solution.py:10
  26.9 296.6 %all-gather.11.cloned.1.call-start = ((), (), s32[]{:S(2)}) async-start(), calls=%async_computation.3 | async-start | bytes 8912896 | tf_op jit(solution)/shard_map/all_gather | solution.py:10
  253.2 74.9 %copy-start = (f32[4,32,4096]{2,1,0:T(8,128)S(1)}, f32[4,32,4096]{2,1,0:T(8,128)}, u32[]{:S(2)}) copy-start(f32[4,32,4096]{2,1,0:T(8,128)} %param.10) | copy-start | bytes 6291460
Sparse Core Ops, SparseCore 0:
  21.2 76.0 all-gather.8
  100.0 72.8 all-gather.4
  175.6 72.8 all-gather.6
  250.6 72.8 all-gather.10
